TPU v7x, 32 devices: a whole 2x2x4 slice. The times are simulated.
32 devices in a mesh: prow: 4 (over z), pcol: 8 (over y, x, core).
Axes of the slice: x: 2, y: 2, z: 4, core: 2. Of those that a mesh axis runs over, the one named last changes fastest.
Arguments:
- site_code: int32 [17408], P(('prow', 'pcol')), may hold values from 0 to 285212671, as said below
- length_scale: float32 [1], replicated, may hold values from 6 to 12
- noise_var: float32 [1], replicated, may hold values from 0.3 to 1
Outputs:
- panel: bfloat16 [16, 1024, 1024], P('prow')
- trailing: bfloat16 [16, 1024, 8, 1024], P('prow', None, 'pcol')
Inputs may be any that keep to these rules, and one draw needn't show every extreme that they name: `site_code`: each entry is 128 * 128 * s + 128 * x + y for a slot s and bins x, y in 0 .. 127; every slot of 0 .. 17407 appears once. With b = s // 1024 and r = s mod 1024, the home of slot s is the device of prow-major index r mod (32) if b = 0, else the device (prow (b - 1) mod 4, pcol r mod 8); no device holds more than 17 sites of one home, and some device holds exactly 17 sites of some home.
All inputs are finite; a program needn't handle non-finite values.
Results may differ from a plain program's by a relative error of at most 0.0036.
Values may be sent and summed in bfloat16 or wider, within the bound.
No kernel may reach another device: no remote copies, remote signals or barrier semaphores. Data moves between devices by JAX's collectives and lax.ppermute only.
A program may use at most 192 MiB of HBM per device.

v0:
```python
import jax
import jax.numpy as jnp
from jax import lax
from jax.sharding import PartitionSpec as P

B = 1024
GRID = 128
TR_DEV = 4
SLAB_DEV = 1


def from_root(value, axis, source):
    kept = jnp.where(lax.axis_index(axis) == source, value, 0).astype(value.dtype)
    return lax.psum(kept, axis)


def site_features(codes):
    coord_x = (codes // GRID % GRID).astype(jnp.float32)
    coord_y = (codes % GRID).astype(jnp.float32)
    radius_sq = coord_x * coord_x + coord_y * coord_y
    ones = jnp.ones_like(coord_x)
    left = jnp.stack([coord_x, coord_y, radius_sq, ones], -2)
    right = jnp.stack([-2.0 * coord_x, -2.0 * coord_y, ones, radius_sq], -2)
    return (left, right)


def cov_tile(left, right, decay_rate, nugget, same):
    squared = jnp.einsum("...ka,kb->...ab", left, right, precision=lax.Precision.HIGHEST)
    distance = jnp.sqrt(jnp.maximum(squared, 0.0))
    scaled = decay_rate * distance
    values = (1.0 + scaled) * jnp.exp(-scaled)
    rank_count = values.ndim
    eye_mask = lax.broadcasted_iota(
        jnp.int32, values.shape, rank_count - 2
    ) == lax.broadcasted_iota(jnp.int32, values.shape, rank_count - 1)
    return values + jnp.where(eye_mask, nugget * same, 0.0)


def body(site_code, length_scale, noise_var):
    n_prow = lax.axis_size("prow")
    n_pcol = lax.axis_size("pcol")
    devices = n_prow * n_pcol
    me_row = lax.axis_index("prow")
    me_col = lax.axis_index("pcol")
    decay_rate = jnp.sqrt(3.0) / length_scale[0]
    nugget = noise_var[0]
    pick_index = me_col // n_prow + jnp.arange(SLAB_DEV, dtype=jnp.int32) * (n_pcol // n_prow)
    capacity = (TR_DEV * B // n_pcol + B // devices + devices - 1) // devices
    site_slot = site_code // (GRID * GRID)
    block_id = site_slot // B
    block_pos = site_slot % B
    home_dev = jnp.where(
        block_id == 0, block_pos % devices, (block_id - 1) % n_prow * n_pcol + block_pos % n_pcol
    )
    one_hot = (home_dev[:, None] == jnp.arange(devices, dtype=jnp.int32)[None, :]).astype(jnp.int32)
    arrival_rank = jnp.sum(jnp.cumsum(one_hot, axis=0) * one_hot, axis=1) - 1
    outbox = jnp.full((devices, capacity), -1, jnp.int32).at[home_dev, arrival_rank].set(site_code)
    inbox = lax.all_to_all(
        outbox, ("prow", "pcol"), split_axis=0, concat_axis=0, tiled=True
    ).reshape(-1)
    valid = inbox >= 0
    got_slot = jnp.where(valid, inbox // (GRID * GRID), 0)
    got_block = got_slot // B
    got_pos = got_slot % B
    row_width = B // n_pcol
    tile_index = jnp.where(valid & (got_block > 0), (got_block - 1) // n_prow, TR_DEV)
    row_home = (
        jnp.full((TR_DEV, row_width), -1, jnp.int32)
        .at[tile_index, got_pos // n_pcol]
        .set(inbox, mode="drop")
    )
    panel_width = B // devices
    panel_index = jnp.where(valid & (got_block == 0), got_pos // devices, panel_width)
    panel_home = jnp.full((panel_width,), -1, jnp.int32).at[panel_index].set(inbox, mode="drop")
    row_all = lax.all_gather(row_home, "pcol", axis=1, tiled=True)
    row_codes = row_all.reshape(TR_DEV, n_pcol, row_width).transpose(0, 2, 1).reshape(TR_DEV, B)
    panel_all = lax.all_gather(panel_home, ("prow", "pcol"), axis=0, tiled=True)
    panel_codes = panel_all.reshape(devices, panel_width).T.reshape(B)
    col_codes = from_root(jnp.take(row_codes, pick_index, axis=0), "prow", me_col % n_prow)
    panel_left, panel_right = site_features(panel_codes)
    row_left, row_right = site_features(row_codes)
    col_left, col_right = site_features(col_codes)

    def factor_panel(unused):
        diag_factor = jnp.linalg.cholesky(
            cov_tile(panel_left, panel_right, decay_rate, nugget, 1.0)
        )
        tiles = cov_tile(row_left, panel_right, decay_rate, nugget, 0.0)
        solved = jax.scipy.linalg.solve_triangular(
            diag_factor, tiles.reshape(TR_DEV * B, B).T, lower=True
        )
        return solved.T.reshape(TR_DEV, B, B).astype(jnp.bfloat16)

    def skip_panel(unused):
        return jnp.zeros((TR_DEV, B, B), jnp.bfloat16)

    panel_mine = lax.cond(me_col == 0, factor_panel, skip_panel, 0)
    panel_rows = from_root(panel_mine, "pcol", 0)
    panel_pick = jnp.take(panel_rows, pick_index, axis=0)
    panel_cols = from_root(panel_pick, "prow", me_col % n_prow)
    row_results = []
    for row_tile in range(TR_DEV):
        trail = row_tile * n_prow + me_row
        other = 0 + me_col
        same = jnp.where(trail == other, 1.0, 0.0)
        tile = cov_tile(row_left[row_tile], col_right[0], decay_rate, nugget, same)
        product = lax.dot_general(
            panel_rows[row_tile],
            panel_cols[0],
            (((1,), (1,)), ((), ())),
            preferred_element_type=jnp.float32,
        )
        col_results = [(tile - product).astype(jnp.bfloat16)]
        row_results.append(jnp.stack(col_results, 1))
    trailing = jnp.stack(row_results, 0)
    return (panel_rows, trailing)


def solution(mesh):
    in_specs = (P(("prow", "pcol")), P(), P())
    out_specs = (P("prow", None, None), P("prow", None, "pcol", None))
    return jax.shard_map(body, mesh=mesh, in_specs=in_specs, out_specs=out_specs, check_vma=False)
```

profile of v0, /device:TPU:0, one launch (start us, length us, event | category | flops | bytes accessed | tf_op | source)
XLA Modules:
  0.0 914.6 jit_solution(17226715184799600394)
XLA Ops:
  9.8 46.5 %scatter_fusion = s32[32,17]{0,1:T(8,128)S(1)} fusion(s32[32,17]{0,1:T(8,128)S(1)} %broadcast_in_dim.85, s32[544]{0:T(1024)S(1)} %fusion.113, s32[544]{0:T(1024)} %param.5), kind=kCustom, calls=%fused_computation | custom fusion | bytes 10880 | tf_op jit(solution)/shard_map/scatter | solution.py:57
  57.1 7.3 all-to-all-start
  65.2 6.3 all-to-all-done
  73.1 25.6 %scatter_fusion.1 = s32[4,128]{1,0:T(4,128)S(1)} fusion(s32[4,128]{1,0:T(4,128)S(1)} %broadcast_in_dim.87, s32[544]{0:T(1024)S(1)} %get-tuple-element.66, s32[544]{0:T(1024)S(1)} %reshape.975), kind=kCustom, calls=%fused_computation.2 | custom fusion | bytes 10880 | tf_op jit(solution)/shard_map/scatter | solution.py:70
  98.7 8.0 all_gather.7
  107.0 4.1 scatter_custom_fusion.1
  111.4 38.2 %all-reduce.2 = s32[1024]{0:T(1024)S(1)} all-reduce(s32[1024]{0:T(1024)S(1)} %dynamic-update-slice.49), channel_id=1, replica_groups=mesh['prow'=4,'pcol'=8] {'prow','pcol'}, use_global_device_ids=true, to_apply=%add.2 | all-reduce | flops 1024 | bytes 8192
  150.1 487.1 %conditional.1 = (bf16[4,1024,1024]{2,1,0:T(8,128)(2,1)}) conditional(s32[]{:T(128)} %convert_element_type.98, () %tuple.14, (f32[]{:T(128)}, f32[4,1024]{1,0:T(4,128)S(1)}, f32[4,1024]{1,0:T(4,128)S(1)}, f32[]{:T(128)}, f32[4,4,1024]{2,0,1:T(4,128)S(1)}) %tuple.15), branch_computations={%region_6.7_spmd, %region_7.24_spmd} | conditional | flops 32137316352 | bytes 414441856 | solution.py:97
  150.8 3.5 fusion.125
  156.2 3.8 fusion.24
  160.0 5.5 copy.27
  165.5 6.3 add_multiply_fusion
  173.8 11.7 %cholesky.5 = f32[128,128]{1,0:T(8,128)S(1)} custom-call(f32[128,128]{1,0:T(8,128)S(1)} %cholesky.221), custom_call_target="Cholesky" | custom-call | tf_op jit(solution)/shard_map/cond/branch_1_fun/jit(cholesky)/cholesky | solution.py:85
  185.5 9.8 %custom-call.55 = f32[1,128,128]{1,2,0:T(8,128)S(1)} custom-call(f32[1,128,128]{2,1,0:T(8,128)S(1)} %get-tuple-element.130), custom_call_target="InvertDiagBlocksLowerTriangular" | custom-call | tf_op jit(solution)/shard_map/cond/branch_1_fun/jit(cholesky)/cholesky | solution.py:85
  201.8 12.1 %cholesky.27 = f32[128,128]{1,0:T(8,128)S(1)} custom-call(f32[128,128]{1,0:T(8,128)S(1)} %cholesky.227), custom_call_target="Cholesky" | custom-call | tf_op jit(solution)/shard_map/cond/branch_1_fun/jit(cholesky)/cholesky | solution.py:85
  216.5 9.8 %custom-call.56 = f32[1,128,128]{1,2,0:T(8,128)S(1)} custom-call(f32[1,128,128]{2,1,0:T(8,128)S(1)} %get-tuple-element.127), custom_call_target="InvertDiagBlocksLowerTriangular" | custom-call | tf_op jit(solution)/shard_map/cond/branch_1_fun/jit(cholesky)/cholesky | solution.py:85
  229.6 11.7 %cholesky.58 = f32[128,128]{1,0:T(8,128)S(1)} custom-call(f32[128,128]{1,0:T(8,128)S(1)} %cholesky.232), custom_call_target="Cholesky" | custom-call | tf_op jit(solution)/shard_map/cond/branch_1_fun/jit(cholesky)/cholesky | solution.py:85
  243.4 9.8 %custom-call.57 = f32[1,128,128]{1,2,0:T(8,128)S(1)} custom-call(f32[1,128,128]{2,1,0:T(8,128)S(1)} %get-tuple-element.124), custom_call_target="InvertDiagBlocksLowerTriangular" | custom-call | tf_op jit(solution)/shard_map/cond/branch_1_fun/jit(cholesky)/cholesky | solution.py:85
  256.9 11.7 %cholesky.87 = f32[128,128]{1,0:T(8,128)S(1)} custom-call(f32[128,128]{1,0:T(8,128)S(1)} %cholesky.237), custom_call_target="Cholesky" | custom-call | tf_op jit(solution)/shard_map/cond/branch_1_fun/jit(cholesky)/cholesky | solution.py:85
  270.7 9.8 %custom-call.58 = f32[1,128,128]{1,2,0:T(8,128)S(1)} custom-call(f32[1,128,128]{2,1,0:T(8,128)S(1)} %get-tuple-element.121), custom_call_target="InvertDiagBlocksLowerTriangular" | custom-call | tf_op jit(solution)/shard_map/cond/branch_1_fun/jit(cholesky)/cholesky | solution.py:85
  283.9 11.7 %cholesky.116 = f32[128,128]{1,0:T(8,128)S(1)} custom-call(f32[128,128]{1,0:T(8,128)S(1)} %cholesky.242), custom_call_target="Cholesky" | custom-call | tf_op jit(solution)/shard_map/cond/branch_1_fun/jit(cholesky)/cholesky | solution.py:85
  297.7 10.2 %custom-call.59 = f32[1,128,128]{1,2,0:T(8,128)S(1)} custom-call(f32[1,128,128]{2,1,0:T(8,128)S(1)} %get-tuple-element.118), custom_call_target="InvertDiagBlocksLowerTriangular" | custom-call | tf_op jit(solution)/shard_map/cond/branch_1_fun/jit(cholesky)/cholesky | solution.py:85
  311.1 11.7 %cholesky.146 = f32[128,128]{1,0:T(8,128)S(1)} custom-call(f32[128,128]{1,0:T(8,128)S(1)} %cholesky.249), custom_call_target="Cholesky" | custom-call | tf_op jit(solution)/shard_map/cond/branch_1_fun/jit(cholesky)/cholesky | solution.py:85
  324.9 9.8 %custom-call.60 = f32[1,128,128]{1,2,0:T(8,128)S(1)} custom-call(f32[1,128,128]{2,1,0:T(8,128)S(1)} %get-tuple-element.115), custom_call_target="InvertDiagBlocksLowerTriangular" | custom-call | tf_op jit(solution)/shard_map/cond/branch_1_fun/jit(cholesky)/cholesky | solution.py:85
  337.7 11.9 %cholesky.176 = f32[128,128]{1,0:T(8,128)S(1)} custom-call(f32[128,128]{1,0:T(8,128)S(1)} %cholesky.256), custom_call_target="Cholesky" | custom-call | tf_op jit(solution)/shard_map/cond/branch_1_fun/jit(cholesky)/cholesky | solution.py:85
  351.6 9.8 %custom-call.61 = f32[1,128,128]{1,2,0:T(8,128)S(1)} custom-call(f32[1,128,128]{2,1,0:T(8,128)S(1)} %get-tuple-element.112), custom_call_target="InvertDiagBlocksLowerTriangular" | custom-call | tf_op jit(solution)/shard_map/cond/branch_1_fun/jit(cholesky)/cholesky | solution.py:85
  364.0 11.7 %cholesky.204 = f32[128,128]{1,0:T(8,128)S(1)} custom-call(f32[128,128]{1,0:T(8,128)S(1)} %convolution_subtract_fusion.11), custom_call_target="Cholesky" | custom-call | tf_op jit(solution)/shard_map/cond/branch_1_fun/jit(cholesky)/cholesky | solution.py:85
  377.7 4.9 select_select_fusion
  382.6 24.1 %while.3 = (s32[]{:T(128)}, f32[1024,1024]{1,0:T(8,128)}, s32[8,2]{0,1:T(2,128)S(1)}, f32[8,128,128]{2,1,0:T(8,128)S(1)}, s32[]{:T(128)}) while((s32[]{:T(128)}, f32[1024,1024]{1,0:T(8,128)}, s32[8,2]{0,1:T(2,128)S(1)}, f32[8,128,128]{2,1,0:T(8,128)S(1)}, s32[]{:T(128)}) %tuple.95), condition=%wide.while_cond, body=%wide.while_body.sunk | while | flops 2 | bytes 131189 | solution.py:89
  406.7 78.6 %custom-call.62 = f32[8,128,128]{1,2,0:T(8,128)S(1)} custom-call(f32[8,128,128]{2,1,0:T(8,128)S(1)} %get-tuple-element.27), custom_call_target="InvertDiagBlocksLowerTriangular" | custom-call | tf_op jit(solution)/shard_map/cond/branch_1_fun/jit(_solve_triangular)/triangular_solve | solution.py:89
  485.3 23.3 %select_add_fusion = f32[4,1024,1024]{2,1,0:T(8,128)} fusion(f32[]{:T(128)S(6)} %mul.122, f32[]{:T(128)} %get-tuple-element.4, f32[4,4,1024]{2,0,1:T(4,128)S(1)} %get-tuple-element.64, f32[4,1024]{1,0:T(4,128)S(1)} %get-tuple-element.15), kind=kOutput, calls=%fused_computation.5 | convolution fusion | flops 234881024 | bytes 16859144 | tf_op jit(solution)/shard_map/cond/branch_1_fun/...ka,kb->...ab/dot_general | solution.py:28
  508.6 17.9 %copy.28 = f32[4096,1024]{0,1:T(8,128)} copy(f32[4096,1024]{1,0:T(8,128)} %bitcast.202) | data formatting | bytes 33554432 | tf_op jit(solution)/shard_map/cond/branch_1_fun/reshape | solution.py:90
  526.5 4.6 convert_dynamic-update-slice_fusion.6
  531.1 4.3 convolution_subtract_fusion.3
  535.4 2.9 convert_dynamic-update-slice_fusion.5
  538.4 3.3 convolution_subtract_fusion.2
  544.6 5.0 fusion.14
  549.6 2.9 convert_dynamic-update-slice_fusion.3
  552.5 7.3 fusion.17
  559.7 4.5 convert_dynamic-update-slice_fusion.2
  564.2 3.4 constant_dynamic-update-slice_fusion.17
  567.6 3.4 constant_dynamic-update-slice_fusion.16
  571.0 3.5 constant_dynamic-update-slice_fusion.15
  574.4 3.4 constant_dynamic-update-slice_fusion.14
  577.8 3.6 constant_dynamic-update-slice_fusion.13
  581.4 9.1 convolution_subtract_fusion.1
  590.6 2.9 convert_dynamic-update-slice_fusion.1
  596.0 9.8 %convolution_subtract_fusion = f32[128,4096]{1,0:T(8,128)S(1)} fusion(f32[768,4096]{1,0:T(8,128)} %get-tuple-element.93, f32[1024,4096]{1,0:T(8,128)S(1)} %bitcast.200, f32[1024,1024]{1,0:T(8,128)} %get-tuple-element.212), kind=kOutput, calls=%fused_computation.21 | convolution fusion | flops 4832362496 | bytes 17170432 | tf_op jit(solution)/shard_map/cond/branch_1_fun/jit(_solve_triangular)/triangular_solve | solution.py:89
  605.8 2.9 convert_dynamic-update-slice_fusion
  610.3 12.0 %convolution_subtract_fusion.4 = f32[128,4096]{1,0:T(8,128)S(1)} fusion(f32[896,4096]{1,0:T(8,128)} %constant_dynamic-update-slice_fusion.11, f32[1024,4096]{1,0:T(8,128)S(1)} %bitcast.201, f32[1024,1024]{1,0:T(8,128)} %get-tuple-element.212), kind=kOutput, calls=%fused_computation.25 | convolution fusion | flops 5637668864 | bytes 19333120 | tf_op jit(solution)/shard_map/cond/branch_1_fun/jit(_solve_triangular)/triangular_solve | solution.py:89
  625.1 11.9 %copy.38 = bf16[4096,1024]{1,0:T(8,128)(2,1)} copy(bf16[4096,1024]{0,1:T(8,128)(2,1)} %bitcast.26) | data formatting | bytes 16777216 | tf_op jit(solution)/shard_map/cond | solution.py:97
  637.2 7.3 broadcast_select_fusion
  644.7 123.6 %all-reduce.6.cloned.1.call-done = bf16[4,1024,1024]{2,1,0:T(8,128)(2,1)} async-done(((bf16[4,1024,1024]{2,1,0:T(8,128)(2,1)}), bf16[4,1024,1024]{2,1,0:T(8,128)(2,1)}) %all-reduce.6.cloned.1.call-update) | async-done | bytes 8388624 | tf_op jit(solution)/shard_map/psum | solution.py:14
  768.2 3.1 fusion.77
  772.3 8.4 psum.22
  780.8 76.9 %all-reduce.8.cloned.1.call-done = bf16[1024,1024]{1,0:T(8,128)(2,1)} async-done(((bf16[1024,1024]{1,0:T(8,128)(2,1)}), bf16[1024,1024]{1,0:T(8,128)(2,1)}) %all-reduce.8.cloned.1.call-update) | async-done | bytes 2097168 | tf_op jit(solution)/shard_map/psum | solution.py:14
  857.8 4.6 fusion.72
  862.4 6.1 fusion.81
  868.5 4.1 fusion.73
  872.6 6.1 fusion.80
  881.1 6.3 fusion.79
  889.8 6.1 fusion.78
  895.9 3.9 pad_maximum_fusion
  899.8 7.8 copy.122
  (129 shorter events, 84.0 us)
Async XLA Ops:
  57.1 14.4 %all-to-all-start = ((s32[32,1,17]{2,1,0:T(1,128)}), s32[32,1,17]{2,1,0:T(1,128)S(1)}, u32[]{:S(2)}, u32[]{:S(2)}) async-start(s32[32,1,17]{2,1,0:T(1,128)} %copy.31), calls=%async_computation | async-start | bytes 32768 | tf_op jit(solution)/shard_map/all_to_all | solution.py:58
  64.4 703.8 %all-reduce.6.cloned.1.call-start = ((), (), s32[]{:S(2)}) async-start(), calls=%async_computation.1 | async-start | bytes 16777216 | tf_op jit(solution)/shard_map/psum | solution.py:14
  154.3 1.9 copy-start.1
  171.8 2.0 copy-start.2
  526.5 11.9 %copy-start = (f32[4096,1024]{0,1:T(8,128)S(1)}, f32[4096,1024]{0,1:T(8,128)}, u32[]{:S(2)}) copy-start(f32[4096,1024]{0,1:T(8,128)} %copy.28) | copy-start | bytes 50331652 | tf_op jit(solution)/shard_map/cond
  644.6 213.2 %all-reduce.8.cloned.1.call-start = ((), (), s32[]{:S(2)}) async-start(), calls=%async_computation.2 | async-start | bytes 4194304 | tf_op jit(solution)/shard_map/psum | solution.py:14
  862.4 6.1 copy-start.3
  862.4 16.3 %slice-start = ((s8[8388608]{0:T(1024)(128)(4,1)}), s8[4194304]{0:T(1024)(128)(4,1)S(1)}, s32[]{:S(2)}) async-start(s8[8388608]{0:T(1024)(128)(4,1)} %bitcast.203), calls=%async_computation.3 | async-start | bytes 8388608
  868.5 10.2 %slice-start.1 = ((s8[8388608]{0:T(1024)(128)(4,1)}), s8[4194304]{0:T(1024)(128)(4,1)S(1)}, s32[]{:S(2)}) async-start(s8[8388608]{0:T(1024)(128)(4,1)} %bitcast.203), calls=%async_computation.4 | async-start | bytes 8388608
Sparse Core Ops, SparseCore 0:
  644.7 123.4 all-reduce.5
  771.5 86.2 all-reduce.7
where the time goes:
time: 926 us; the launch traced here: 915 us
  other arithmetic  284 us (31%)
  waiting for transfers between devices  207 us (22%)
  local copies, waits for them, and re-layouts  174 us (19%)
  matrix products  165 us (18%)
  blocking collectives  54.6 us (6%)
  between operations  16 us (2%)
    psum x2, waiting for transfers between devices, from_root(): return lax.psum(kept, axis)  201 us
    another operation x30, other arithmetic, factor_panel(): jnp.linalg.cholesky(cov_tile(panel_left, panel_right, decay_rate, nugget,...  173 us
    another operation x3, other arithmetic, factor_panel(): jax.scipy.linalg.solve_triangular(diag_factor, tiles.reshape(TR_DEV * B,...  83.5 us
    another operation x15, matrix products, factor_panel(): jax.scipy.linalg.solve_triangular(diag_factor, tiles.reshape(TR_DEV * B,...  77.3 us
    dot_general x6, matrix products, cov_tile(): jnp.einsum('...ka,kb->...ab', left, right, precision=lax.Precision.HIGHEST)  51.4 us
    scatter x1, local copies, waits for them, and re-layouts, body(): jnp.full((devices, capacity), -1, jnp.int32).at[home_dev, arrival_rank]  46.5 us
    unnamed x1, blocking collectives  38.2 us
    scatter x1, local copies, waits for them, and re-layouts, body(): row_home = jnp.full((TR_DEV, row_width), -1, jnp.int32).at[tile_index, go...  25.6 us
  transfers between devices with their start and end apart: 3, of which 3 were waited for; matrix products, arithmetic and copies ran while one was open for 0% of the time, Pallas kernels for 0%

commit v1 on v0

v1 whole, which is shorter than its diff:
```python
import functools

import jax
import jax.numpy as jnp
from jax import lax
from jax.experimental import pallas as pl
from jax.experimental.pallas import tpu as pltpu
from jax.sharding import PartitionSpec as P

B = 1024
GRID = 128
TR_DEV = 4
SLAB_DEV = 1
LANES = 128
SUB = 8
NB = 128
STRIP = 256
F32 = jnp.float32
BF16 = jnp.bfloat16
NN = (((1,), (0,)), ((), ()))
NT = (((1,), (1,)), ((), ()))


def split(value):
    high = value.astype(BF16)
    return high, (value - high.astype(F32)).astype(BF16)


def dot(a, b, dims):
    return lax.dot_general(a, b, dims, preferred_element_type=F32)


def dot3(a, b, dims):
    (a_high, a_low), (b_high, b_low) = a, b
    return dot(a_high, b_high, dims) + (dot(a_high, b_low, dims) + dot(a_low, b_high, dims))


def matern(squared, decay_sq):
    scaled_sq = squared * decay_sq
    scaled = scaled_sq * lax.rsqrt(jnp.maximum(scaled_sq, 1e-30))
    return (1.0 + scaled) * jnp.exp(-scaled)


def row_of(value, index):
    return jnp.broadcast_to(value[index : index + 1, :], value.shape)


def lane_of(value, index):
    return jnp.broadcast_to(value[:, index : index + 1], value.shape)


def order_sites(codes_ref, blocks_ref, left_ref, right_ref, n_blocks):
    n_rows, width = codes_ref.shape
    per_block = B // LANES
    n_high = n_blocks * per_block
    sub = lax.broadcasted_iota(jnp.int32, (n_high, width), 0)
    target = jnp.zeros((n_high, width), jnp.int32)
    for b in range(n_blocks):
        target = jnp.where(sub // per_block == b, blocks_ref[b] * per_block + sub % per_block, target)
    low_iota = lax.broadcasted_iota(jnp.int32, (LANES, width), 0)

    def add_rows(step, total):
        codes = codes_ref[pl.ds(pl.multiple_of(step * SUB, SUB), SUB), :]
        slot = codes >> 14
        high = slot >> 7
        low = slot & (LANES - 1)
        x = ((codes >> 7) & (GRID - 1)).astype(F32)
        y = (codes & (GRID - 1)).astype(F32)
        for r in range(SUB):
            mine = target == high[r : r + 1, :]
            lhs_x = jnp.where(mine, x[r : r + 1, :], 0.0)
            lhs_y = jnp.where(mine, y[r : r + 1, :], 0.0)
            lhs = jnp.concatenate([lhs_x, lhs_y], 0).astype(BF16)
            rhs = jnp.where(low_iota == low[r : r + 1, :], 1.0, 0.0).astype(BF16)
            total = total + dot(lhs, rhs, NT)
        return total

    total = lax.fori_loop(0, n_rows // SUB, add_rows, jnp.zeros((2 * n_high, LANES), F32))
    x_all, y_all = total[:n_high], total[n_high:]
    radius_sq = x_all * x_all + y_all * y_all
    radius_high = jnp.floor(radius_sq * (1.0 / 256.0)) * 256.0
    radius_low = radius_sq - radius_high
    feature = lax.broadcasted_iota(jnp.int32, (2 * SUB, LANES), 0)

    def stack(rows):
        tile = jnp.zeros((2 * SUB, LANES), F32)
        for f, row in enumerate(rows):
            tile = jnp.where(feature == f, row, tile)
        return tile

    for h in range(n_high):
        x, y = x_all[h : h + 1], y_all[h : h + 1]
        rh, rl = radius_high[h : h + 1], radius_low[h : h + 1]
        right = stack([x, y, 1.0, 1.0, rh, rl])
        left = stack([-2.0 * x, -2.0 * y, rh, rl, 1.0, 1.0])
        right_ref[:, LANES * h : LANES * (h + 1)] = right.astype(BF16)
        left_ref[LANES * h : LANES * (h + 1), :] = jnp.transpose(left).astype(BF16)


def eliminate(rows, e):
    sub = lax.broadcasted_iota(jnp.int32, (SUB, LANES), 0)
    e = list(e)
    for s in range(0, SUB, 2):
        a, b, c = row_of(e[s], s), row_of(e[s + 1], s), row_of(e[s + 1], s + 1)
        inverse = 1.0 / (a * c - b * b)
        first = jnp.where(sub == s, -1.0, jnp.where(sub == s + 1, 0.0, e[s]))
        second = jnp.where(sub == s + 1, -1.0, jnp.where(sub == s, 0.0, e[s + 1]))
        pair = (sub == s) | (sub == s + 1)

        def reduced(z):
            u, v = row_of(z, s), row_of(z, s + 1)
            change = first * (c * u - b * v) + second * (a * v - b * u)
            return jnp.where(pair, 0.0, z) - change * inverse

        rows = [reduced(z) for z in rows]
        for t in range(s + 2, SUB):
            e[t] = reduced(e[t])
    return rows


def small_inverse_factor(d):
    sub = lax.broadcasted_iota(jnp.int32, (SUB, LANES), 0)
    d = list(d)
    z = [jnp.where(sub == j, 1.0, 0.0) for j in range(SUB)]
    for s in range(SUB):
        scale = lax.rsqrt(row_of(d[s], s))
        col = d[s] * scale
        below = jnp.where(sub > s, col, 0.0)
        for t in range(s + 1, SUB):
            d[t] = d[t] - below * row_of(col, t)
        for j in range(s + 1):
            pivot = row_of(z[j], s) * scale
            z[j] = jnp.where(sub == s, pivot, z[j] - below * pivot)
    return z


def factor_block(s_ref, b_ref, w_ref):
    groups = NB // SUB
    row = lax.broadcasted_iota(jnp.int32, (NB, NB), 0)
    col = lax.broadcasted_iota(jnp.int32, (NB, NB), 1)
    b_ref[...] = jnp.where(row == col, 1.0, 0.0)
    lane = lax.broadcasted_iota(jnp.int32, (SUB, LANES), 1)
    diag = [jnp.where(lax.broadcasted_iota(jnp.int32, (SUB, LANES), 0) == s, 1.0, 0.0) for s in range(SUB)]
    for p in range(groups):
        rows = slice(SUB * p, SUB * (p + 1))
        s_rows, b_rows = s_ref[rows, :], b_ref[rows, :]
        e = [lane_of(s_rows, SUB * p + s) for s in range(SUB)]
        diag = [jnp.where(lane == p, e[s], diag[s]) for s in range(SUB)]
        if p == groups - 1:
            break
        q_s, q_b = eliminate([s_rows, b_rows], e)
        q_s = [row_of(q_s, s) for s in range(SUB)]
        q_b = [row_of(q_b, s) for s in range(SUB)]
        for g in range(p + 1, groups):
            other = slice(SUB * g, SUB * (g + 1))
            s_old, b_old = s_ref[other, :], b_ref[other, :]
            m = [lane_of(s_old, SUB * p + s) for s in range(SUB)]
            terms_s = [m[s] * q_s[s] for s in range(SUB)]
            terms_b = [m[s] * q_b[s] for s in range(SUB)]
            while len(terms_s) > 1:
                terms_s = [u + v for u, v in zip(terms_s[::2], terms_s[1::2])]
                terms_b = [u + v for u, v in zip(terms_b[::2], terms_b[1::2])]
            s_ref[other, :] = s_old - terms_s[0]
            b_ref[other, :] = b_old - terms_b[0]
    factor = small_inverse_factor(diag)
    for p in range(groups):
        rows = slice(SUB * p, SUB * (p + 1))
        b_rows = b_ref[rows, :]
        terms = [lane_of(factor[s], p) * row_of(b_rows, s) for s in range(SUB)]
        while len(terms) > 1:
            terms = [u + v for u, v in zip(terms[::2], terms[1::2])]
        w_ref[rows, :] = terms[0]


def factor_diagonal(a_ref, s_ref, b_ref, w_ref, inv_high_ref, inv_low_ref):
    steps = B // NB
    inv_high_ref[...] = jnp.zeros_like(inv_high_ref)
    inv_low_ref[...] = jnp.zeros_like(inv_low_ref)

    def step(k, carry):
        factor_block(s_ref, b_ref, w_ref)
        for c in range(steps):

            @pl.when(k == c)
            def _(c=c):
                lo, hi = c * NB, (c + 1) * NB
                w = w_ref[...]
                w_parts = split(w)
                left = []
                if c:
                    left = [dot3(w_parts, split(a_ref[lo:hi, 0:lo]), NN)]
                inv_row = split(jnp.concatenate(left + [w], 1))
                inv_high_ref[lo:hi, 0:hi] = inv_row[0]
                inv_low_ref[lo:hi, 0:hi] = inv_row[1]
                if hi == B:
                    return
                below = split(dot3(split(a_ref[hi:B, lo:hi]), w_parts, NT))
                for i in range(c + 1, steps):
                    at = (i - c - 1) * NB
                    rows = slice(i * NB, (i + 1) * NB)
                    mine = tuple(part[at : at + NB] for part in below)
                    upto = tuple(part[: at + NB] for part in below)
                    new = a_ref[rows, hi : (i + 1) * NB] - dot3(mine, upto, NT)
                    a_ref[rows, hi : (i + 1) * NB] = new
                    if i == c + 1:
                        s_ref[...] = new
                    change = dot3(mine, inv_row, NN)
                    a_ref[rows, lo:hi] = -change[:, lo:hi]
                    if c:
                        a_ref[rows, 0:lo] = a_ref[rows, 0:lo] - change[:, 0:lo]

        return carry

    lax.fori_loop(0, steps, step, 0)


def kernel(
    blocks_ref, scalars_ref, codes_ref, panel_ref, trailing_ref,
    left_ref, right_ref, a_ref, s_ref, b_ref, w_ref, inv_high_ref, inv_low_ref,
    col_ref, panel_buf, trail_buf, panel_sem, trail_sem,
):
    decay_sq, nugget = scalars_ref[0], scalars_ref[1]
    n_blocks = TR_DEV + 1 + SLAB_DEV
    order_sites(codes_ref, blocks_ref, left_ref, right_ref, n_blocks)

    def make_diagonal(i, carry):
        rows = pl.ds(pl.multiple_of(i * NB, NB), NB)
        tile = matern(dot(left_ref[rows, :], right_ref[:, 0:B], NN), decay_sq)
        row = lax.broadcasted_iota(jnp.int32, (NB, B), 0) + i * NB
        col = lax.broadcasted_iota(jnp.int32, (NB, B), 1)
        a_ref[rows, :] = tile + jnp.where(row == col, nugget, 0.0)
        return carry

    lax.fori_loop(0, B // NB, make_diagonal, 0)
    s_ref[...] = a_ref[0:NB, 0:NB]
    factor_diagonal(a_ref, s_ref, b_ref, w_ref, inv_high_ref, inv_low_ref)

    def panel_strip(start):
        rows = pl.ds(pl.multiple_of(start, STRIP), STRIP)
        parts = split(matern(dot(left_ref[rows, :], right_ref[:, 0:B], NN), decay_sq))
        pieces = []
        for j in range(B // STRIP):
            lo, hi = j * STRIP, (j + 1) * STRIP
            inv = (inv_high_ref[lo:hi, 0:hi], inv_low_ref[lo:hi, 0:hi])
            pieces.append(dot3(tuple(part[:, 0:hi] for part in parts), inv, NT).astype(BF16))
        return jnp.concatenate(pieces, 1)

    first_row = B
    first_col = (1 + TR_DEV) * B

    def column_strip(i, carry):
        col_ref[pl.ds(pl.multiple_of(i * STRIP, STRIP), STRIP), :] = panel_strip(first_col + i * STRIP)
        return carry

    lax.fori_loop(0, B // STRIP, column_strip, 0)
    n_strips = TR_DEV * B // STRIP
    per_block = B // STRIP

    def copies(i):
        slot = i % 2
        rows = pl.ds(pl.multiple_of(i * STRIP, STRIP), STRIP)
        return (
            pltpu.make_async_copy(panel_buf.at[slot], panel_ref.at[rows, :], panel_sem.at[slot]),
            pltpu.make_async_copy(trail_buf.at[slot], trailing_ref.at[rows, :], trail_sem.at[slot]),
        )

    def row_strip(i, carry):
        slot = i % 2

        @pl.when(i >= 2)
        def _():
            for copy in copies(i - 2):
                copy.wait()

        panel = panel_strip(first_row + i * STRIP)
        panel_buf[slot] = panel
        rows = pl.ds(pl.multiple_of(first_row + i * STRIP, STRIP), STRIP)
        tile = matern(dot(left_ref[rows, :], right_ref[:, first_col : first_col + B], NN), decay_sq)
        row = lax.broadcasted_iota(jnp.int32, (STRIP, B), 0) + i % per_block * STRIP
        col = lax.broadcasted_iota(jnp.int32, (STRIP, B), 1)
        same = blocks_ref[1 + i // per_block] == blocks_ref[1 + TR_DEV]
        tile = tile + jnp.where((row == col) & same, nugget, 0.0)
        trail_buf[slot] = (tile - dot(panel, col_ref[...], NT)).astype(BF16)
        for copy in copies(i):
            copy.start()
        return carry

    lax.fori_loop(0, n_strips, row_strip, 0)
    for i in range(n_strips - 2, n_strips):
        for copy in copies(i):
            copy.wait()


def body(site_code, length_scale, noise_var):
    n_prow = lax.axis_size("prow")
    n_pcol = lax.axis_size("pcol")
    devices = n_prow * n_pcol
    me_row = lax.axis_index("prow")
    me_col = lax.axis_index("pcol")
    width = -(-site_code.shape[0] // LANES) * LANES
    mine = jnp.pad(site_code, (0, width - site_code.shape[0]), constant_values=-1)
    codes = lax.all_to_all(
        jnp.broadcast_to(mine[None], (devices, width)),
        ("prow", "pcol"), split_axis=0, concat_axis=0, tiled=True,
    )
    n_blocks = TR_DEV + 1 + SLAB_DEV
    order = jnp.arange(n_blocks, dtype=jnp.int32)
    row_block = (order - 1) * n_prow + me_row + 1
    blocks = jnp.where(order == 0, 0, jnp.where(order <= TR_DEV, row_block, me_col + 1)).astype(jnp.int32)
    decay_rate = jnp.sqrt(3.0) / length_scale[0]
    scalars = jnp.stack([decay_rate * decay_rate, noise_var[0]])
    rows = TR_DEV * B
    smem = pl.BlockSpec(memory_space=pltpu.SMEM)
    panel, trailing = pl.pallas_call(
        kernel,
        out_shape=(jax.ShapeDtypeStruct((rows, B), BF16), jax.ShapeDtypeStruct((rows, B), BF16)),
        in_specs=[smem, smem, pl.BlockSpec(memory_space=pltpu.VMEM)],
        out_specs=(pl.BlockSpec(memory_space=pl.ANY), pl.BlockSpec(memory_space=pl.ANY)),
        scratch_shapes=[
            pltpu.VMEM((n_blocks * B, 2 * SUB), BF16),
            pltpu.VMEM((2 * SUB, n_blocks * B), BF16),
            pltpu.VMEM((B, B), F32),
            pltpu.VMEM((NB, NB), F32),
            pltpu.VMEM((NB, NB), F32),
            pltpu.VMEM((NB, NB), F32),
            pltpu.VMEM((B, B), BF16),
            pltpu.VMEM((B, B), BF16),
            pltpu.VMEM((B, B), BF16),
            pltpu.VMEM((2, STRIP, B), BF16),
            pltpu.VMEM((2, STRIP, B), BF16),
            pltpu.SemaphoreType.DMA((2,)),
            pltpu.SemaphoreType.DMA((2,)),
        ],
        compiler_params=pltpu.CompilerParams(vmem_limit_bytes=60 * 1024 * 1024),
    )(blocks, scalars, codes)
    return panel.reshape(TR_DEV, B, B), trailing.reshape(TR_DEV, B, SLAB_DEV, B)


def solution(mesh):
    in_specs = (P(("prow", "pcol")), P(), P())
    out_specs = (P("prow", None, None), P("prow", None, "pcol", None))
    return jax.shard_map(body, mesh=mesh, in_specs=in_specs, out_specs=out_specs, check_vma=False)
```

time: 926 us -> 103 us (0.11); the launches traced: 915 us -> 103 us
  other arithmetic: 284 us -> 1.16 us
  waiting for transfers between devices: 207 us -> 5.08 us
  local copies, waits for them, and re-layouts: 174 us -> 2 us
  matrix products: 165 us -> 0 us
  Pallas kernels: 0 us -> 84.8 us
  blocking collectives: 54.6 us -> 0 us
  between operations: 16 us -> 2.14 us
    another operation x42 -> x1, other arithmetic: 262 us -> 0.65 us  [body(): scalars = jnp.stack([decay_rate * decay_rate, noise_var[0]])]
    psum x2 -> x0, waiting for transfers between devices: 201 us -> none  [from_root(): return lax.psum(kept, axis)]
    another operation x29 -> x0, matrix products: 100 us -> none  [the longest x15 77.3 us: factor_panel(): jax.scipy.linalg.solve_triangular(diag_factor, tiles.reshape(TR_DEV * B,...]
    pallas_call x0 -> x1, Pallas kernels: none -> 84.8 us  [body(): pl.pallas_call(kernel, out_shape=(jax.ShapeDtypeStruct((rows, B), BF16),...]
    scatter x3 -> x0, local copies, waits for them, and re-layouts: 76.2 us -> none  [the longest x1 46.5 us: body(): jnp.full((devices, capacity), -1, jnp.int32).at[home_dev, arrival_rank]]
    dot_general x10 -> x0, matrix products: 64.8 us -> none  [the longest x6 51.4 us: cov_tile(): jnp.einsum('...ka,kb->...ab', left, right, precision=lax.Precision.HIGHEST)]
    unnamed x1 -> x0, blocking collectives: 38.2 us -> none
    cond x13 -> x0, local copies, waits for them, and re-layouts: 35.6 us -> none
  transfers between devices with their start and end apart: 3 -> 1, of which waited for: 3 -> 1; matrix products, arithmetic and copies ran while one was open for 0% -> 1% of each run, Pallas kernels for 0% -> 0%
where the time goes in v1:
time: 103 us
  Pallas kernels  84.8 us (82%)
  starting transfers between devices  7.33 us (7%)
  waiting for transfers between devices  5.08 us (5%)
  between operations  2.14 us (2%)
  local copies, waits for them, and re-layouts  2 us (2%)
  other arithmetic  1.16 us (1%)
    pallas_call x1, Pallas kernels, body(): pl.pallas_call(kernel, out_shape=(jax.ShapeDtypeStruct((rows, B), BF16),...  84.8 us
    all_to_all x1, starting transfers between devices, body(): lax.all_to_all(jnp.broadcast_to(mine[None], (devices, width)), ('prow', '...  7.33 us
    all_to_all x1, waiting for transfers between devices, body(): lax.all_to_all(jnp.broadcast_to(mine[None], (devices, width)), ('prow', '...  5.08 us
  transfers between devices with their start and end apart: 1, of which 1 were waited for; matrix products, arithmetic and copies ran while one was open for 1% of the time, Pallas kernels for 0%

profile of v1, /device:TPU:0, one launch (start us, length us, event | category | flops | bytes accessed | tf_op | source)
XLA Modules:
  0.0 102.5 jit_solution(1372004896324196383)
XLA Ops:
  0.6 0.7 pad.4
  1.3 0.7 broadcast_in_dim.13
  2.0 7.3 %all-to-all-start = ((s32[32,1,640]{2,1,0:T(1,128)}), s32[32,1,640]{2,1,0:T(1,128)S(1)}, u32[]{:S(2)}, u32[]{:S(2)}) async-start(s32[32,1,640]{2,1,0:T(1,128)} %broadcast_in_dim.13), calls=%async_computation | async-start | bytes 163840 | tf_op jit(solution)/shard_map/all_to_all | solution.py:302
  10.7 0.7 pad_maximum_fusion.scalars_ref
  11.3 0.5 compare_select_fusion.1.blocks_ref
  11.8 5.1 %all-to-all-done = s32[32,1,640]{2,1,0:T(1,128)S(1)} async-done(((s32[32,1,640]{2,1,0:T(1,128)}), s32[32,1,640]{2,1,0:T(1,128)S(1)}, u32[]{:S(2)}, u32[]{:S(2)}) %all-to-all-start) | async-done | bytes 81952 | tf_op jit(solution)/shard_map/all_to_all | solution.py:302
  16.9 0.6 copy.9
  17.5 84.8 %shard_map.50 = (bf16[4096,1024]{1,0:T(8,128)(2,1)}, bf16[4096,1024]{1,0:T(8,128)(2,1)}) custom-call(s32[6]{0:T(128)} %compare_select_fusion.1.blocks_ref, f32[2]{0:T(128)} %pad_maximum_fusion.scalars_ref, s32[32,640]{1,0:T(8,128)} %bitcast.7), custom_call_target="tpu_custom_call" | custom-call | tf_op jit(solution)/shard_map/pallas_call | solution.py:314
Async XLA Ops:
  2.0 14.9 %all-to-all-start = ((s32[32,1,640]{2,1,0:T(1,128)}), s32[32,1,640]{2,1,0:T(1,128)S(1)}, u32[]{:S(2)}, u32[]{:S(2)}) async-start(s32[32,1,640]{2,1,0:T(1,128)} %broadcast_in_dim.13), calls=%async_computation | async-start | bytes 163840 | tf_op jit(solution)/shard_map/all_to_all | solution.py:302

commit v2 on v1

--- a/solution.py
+++ b/solution.py
@@ -46,7 +46,8 @@
 
 
 def lane_of(value, index):
-    return jnp.broadcast_to(value[:, index : index + 1], value.shape)
+    at = jnp.full(value.shape, index, jnp.int32)
+    return jnp.take_along_axis(value, at, axis=1, mode="promise_in_bounds")
 
 
 def order_sites(codes_ref, blocks_ref, left_ref, right_ref, n_blocks):

time: 103 us -> 98.2 us (0.953)
  Pallas kernels: 84.8 us -> 80.4 us
    pallas_call x1, Pallas kernels: 84.8 us -> 80.4 us  [body(): pl.pallas_call(kernel, out_shape=(jax.ShapeDtypeStruct((rows, B), BF16),...]
where the time goes in v2:
time: 98.2 us; the launch traced here: 97.9 us
  Pallas kernels  80.4 us (82%)
  starting transfers between devices  7.33 us (7%)
  waiting for transfers between devices  5.08 us (5%)
  local copies, waits for them, and re-layouts  2 us (2%)
  between operations  1.97 us (2%)
  other arithmetic  1.16 us (1%)
    pallas_call x1, Pallas kernels, body(): pl.pallas_call(kernel, out_shape=(jax.ShapeDtypeStruct((rows, B), BF16),...  80.4 us
    all_to_all x1, starting transfers between devices, body(): lax.all_to_all(jnp.broadcast_to(mine[None], (devices, width)), ('prow', '...  7.33 us
    all_to_all x1, waiting for transfers between devices, body(): lax.all_to_all(jnp.broadcast_to(mine[None], (devices, width)), ('prow', '...  5.08 us
  transfers between devices with their start and end apart: 1, of which 1 were waited for; matrix products, arithmetic and copies ran while one was open for 1% of the time, Pallas kernels for 0%

profile of v2, /device:TPU:0, one launch (start us, length us, event | category | flops | bytes accessed | tf_op | source)
XLA Modules:
  0.0 97.9 jit_solution(3860793783327618002)
XLA Ops:
  0.6 0.7 pad.4
  1.3 0.7 broadcast_in_dim.13
  2.0 7.3 %all-to-all-start = ((s32[32,1,640]{2,1,0:T(1,128)}), s32[32,1,640]{2,1,0:T(1,128)S(1)}, u32[]{:S(2)}, u32[]{:S(2)}) async-start(s32[32,1,640]{2,1,0:T(1,128)} %broadcast_in_dim.13), calls=%async_computation | async-start | bytes 163840 | tf_op jit(solution)/shard_map/all_to_all | solution.py:303
  10.7 0.7 pad_maximum_fusion.scalars_ref
  11.3 0.5 compare_select_fusion.1.blocks_ref
  11.8 5.1 %all-to-all-done = s32[32,1,640]{2,1,0:T(1,128)S(1)} async-done(((s32[32,1,640]{2,1,0:T(1,128)}), s32[32,1,640]{2,1,0:T(1,128)S(1)}, u32[]{:S(2)}, u32[]{:S(2)}) %all-to-all-start) | async-done | bytes 81952 | tf_op jit(solution)/shard_map/all_to_all | solution.py:303
  16.9 0.6 copy.9
  17.5 80.4 %shard_map.50 = (bf16[4096,1024]{1,0:T(8,128)(2,1)}, bf16[4096,1024]{1,0:T(8,128)(2,1)}) custom-call(s32[6]{0:T(128)} %compare_select_fusion.1.blocks_ref, f32[2]{0:T(128)} %pad_maximum_fusion.scalars_ref, s32[32,640]{1,0:T(8,128)} %bitcast.7), custom_call_target="tpu_custom_call" | custom-call | tf_op jit(solution)/shard_map/pallas_call | solution.py:315
Async XLA Ops:
  2.0 14.9 %all-to-all-start = ((s32[32,1,640]{2,1,0:T(1,128)}), s32[32,1,640]{2,1,0:T(1,128)S(1)}, u32[]{:S(2)}, u32[]{:S(2)}) async-start(s32[32,1,640]{2,1,0:T(1,128)} %broadcast_in_dim.13), calls=%async_computation | async-start | bytes 163840 | tf_op jit(solution)/shard_map/all_to_all | solution.py:303

commit v3 on v2

--- a/solution.py
+++ b/solution.py
@@ -14,7 +14,9 @@
 LANES = 128
 SUB = 8
 NB = 128
+PAIR = 2 * NB
 STRIP = 256
+LN2 = 0.6931471805599453
 F32 = jnp.float32
 BF16 = jnp.bfloat16
 NN = (((1,), (0,)), ((), ()))
@@ -35,10 +37,10 @@
     return dot(a_high, b_high, dims) + (dot(a_high, b_low, dims) + dot(a_low, b_high, dims))
 
 
-def matern(squared, decay_sq):
-    scaled_sq = squared * decay_sq
-    scaled = scaled_sq * lax.rsqrt(jnp.maximum(scaled_sq, 1e-30))
-    return (1.0 + scaled) * jnp.exp(-scaled)
+def matern(left_ref, rows, right_ref, cols, decay_sq):
+    w_sq = jnp.maximum(dot(left_ref[rows, :], right_ref[:, cols], NN) * decay_sq, 1e-30)
+    w = w_sq * lax.rsqrt(w_sq)
+    return (1.0 + w * LN2) * jnp.exp2(-w)
 
 
 def row_of(value, index):
@@ -173,51 +175,59 @@
         w_ref[rows, :] = terms[0]
 
 
-def factor_diagonal(a_ref, s_ref, b_ref, w_ref, inv_high_ref, inv_low_ref):
-    steps = B // NB
-    inv_high_ref[...] = jnp.zeros_like(inv_high_ref)
-    inv_low_ref[...] = jnp.zeros_like(inv_low_ref)
-
-    def step(k, carry):
-        factor_block(s_ref, b_ref, w_ref)
-        for c in range(steps):
-
-            @pl.when(k == c)
-            def _(c=c):
-                lo, hi = c * NB, (c + 1) * NB
-                w = w_ref[...]
-                w_parts = split(w)
-                left = []
-                if c:
-                    left = [dot3(w_parts, split(a_ref[lo:hi, 0:lo]), NN)]
-                inv_row = split(jnp.concatenate(left + [w], 1))
-                inv_high_ref[lo:hi, 0:hi] = inv_row[0]
-                inv_low_ref[lo:hi, 0:hi] = inv_row[1]
-                if hi == B:
-                    return
-                below = split(dot3(split(a_ref[hi:B, lo:hi]), w_parts, NT))
-                for i in range(c + 1, steps):
-                    at = (i - c - 1) * NB
-                    rows = slice(i * NB, (i + 1) * NB)
-                    mine = tuple(part[at : at + NB] for part in below)
-                    upto = tuple(part[: at + NB] for part in below)
-                    new = a_ref[rows, hi : (i + 1) * NB] - dot3(mine, upto, NT)
-                    a_ref[rows, hi : (i + 1) * NB] = new
-                    if i == c + 1:
-                        s_ref[...] = new
-                    change = dot3(mine, inv_row, NN)
-                    a_ref[rows, lo:hi] = -change[:, lo:hi]
-                    if c:
-                        a_ref[rows, 0:lo] = a_ref[rows, 0:lo] - change[:, 0:lo]
-
-        return carry
-
-    lax.fori_loop(0, steps, step, 0)
+def rows_of(parts, start, stop):
+    return tuple(part[start:stop] for part in parts)
+
+
+def finish_pair(j, a_ref, s_ref, w_ref, wa_ref, lba_ref, inv_high_ref, inv_low_ref):
+    lo, hi = j * PAIR, (j + 1) * PAIR
+    w_a, w_b = wa_ref[...], w_ref[...]
+    corner = dot3(split(w_b), split(dot3(split(lba_ref[...]), split(w_a), NN)), NN)
+    w = jnp.concatenate([jnp.concatenate([w_a, jnp.zeros_like(w_a)], 1), jnp.concatenate([-corner, w_b], 1)], 0)
+    w_parts = split(w)
+    below = None
+    if hi < B:
+        below = split(dot3(split(a_ref[hi:B, lo:hi]), w_parts, NT))
+        for i in range(j + 1, B // PAIR):
+            top = i * PAIR
+            mine = rows_of(below, top - hi, top - hi + PAIR)
+            upto = rows_of(below, 0, top - hi + PAIR)
+            new = a_ref[top : top + PAIR, hi : top + PAIR] - dot3(mine, upto, NT)
+            a_ref[top : top + PAIR, hi : top + PAIR] = new
+            if i == j + 1:
+                s_ref[...] = new[0:NB, 0:NB]
+    inv_row = w
+    if j:
+        inv_row = jnp.concatenate([dot3(w_parts, split(a_ref[lo:hi, 0:lo]), NN), w], 1)
+    inv_parts = split(inv_row)
+    inv_high_ref[lo:hi, 0:hi] = inv_parts[0]
+    inv_low_ref[lo:hi, 0:hi] = inv_parts[1]
+    if hi < B:
+        for i in range(j + 1, B // PAIR):
+            rows = slice(i * PAIR, (i + 1) * PAIR)
+            change = dot3(rows_of(below, i * PAIR - hi, (i + 1) * PAIR - hi), inv_parts, NN)
+            a_ref[rows, lo:hi] = -change[:, lo:hi]
+            if j:
+                a_ref[rows, 0:lo] = a_ref[rows, 0:lo] - change[:, 0:lo]
+
+
+def at(start):
+    return pl.ds(pl.multiple_of(start, STRIP), STRIP)
+
+
+def panel_strip(left_ref, right_ref, inv_refs, start, decay_sq):
+    parts = split(matern(left_ref, at(start), right_ref, slice(0, B), decay_sq))
+    pieces = []
+    for j in range(B // PAIR):
+        lo, hi = j * PAIR, (j + 1) * PAIR
+        inv = tuple(ref[lo:hi, 0:hi] for ref in inv_refs)
+        pieces.append(dot3(tuple(part[:, 0:hi] for part in parts), inv, NT).astype(BF16))
+    return jnp.concatenate(pieces, 1)
 
 
 def kernel(
     blocks_ref, scalars_ref, codes_ref, panel_ref, trailing_ref,
-    left_ref, right_ref, a_ref, s_ref, b_ref, w_ref, inv_high_ref, inv_low_ref,
+    left_ref, right_ref, a_ref, s_ref, b_ref, w_ref, wa_ref, lba_ref, inv_high_ref, inv_low_ref,
     col_ref, panel_buf, trail_buf, panel_sem, trail_sem,
 ):
     decay_sq, nugget = scalars_ref[0], scalars_ref[1]
@@ -226,31 +236,41 @@
 
     def make_diagonal(i, carry):
         rows = pl.ds(pl.multiple_of(i * NB, NB), NB)
-        tile = matern(dot(left_ref[rows, :], right_ref[:, 0:B], NN), decay_sq)
         row = lax.broadcasted_iota(jnp.int32, (NB, B), 0) + i * NB
         col = lax.broadcasted_iota(jnp.int32, (NB, B), 1)
+        tile = matern(left_ref, rows, right_ref, slice(0, B), decay_sq)
         a_ref[rows, :] = tile + jnp.where(row == col, nugget, 0.0)
         return carry
 
     lax.fori_loop(0, B // NB, make_diagonal, 0)
     s_ref[...] = a_ref[0:NB, 0:NB]
-    factor_diagonal(a_ref, s_ref, b_ref, w_ref, inv_high_ref, inv_low_ref)
-
-    def panel_strip(start):
-        rows = pl.ds(pl.multiple_of(start, STRIP), STRIP)
-        parts = split(matern(dot(left_ref[rows, :], right_ref[:, 0:B], NN), decay_sq))
-        pieces = []
-        for j in range(B // STRIP):
-            lo, hi = j * STRIP, (j + 1) * STRIP
-            inv = (inv_high_ref[lo:hi, 0:hi], inv_low_ref[lo:hi, 0:hi])
-            pieces.append(dot3(tuple(part[:, 0:hi] for part in parts), inv, NT).astype(BF16))
-        return jnp.concatenate(pieces, 1)
-
+
+    def leaf(index, carry):
+        factor_block(s_ref, b_ref, w_ref)
+        for j in range(B // PAIR):
+            lo, mid, hi = j * PAIR, j * PAIR + NB, (j + 1) * PAIR
+
+            @pl.when(index == 2 * j)
+            def _(lo=lo, mid=mid, hi=hi):
+                w_a = w_ref[...]
+                wa_ref[...] = w_a
+                l_ba = dot3(split(a_ref[mid:hi, lo:mid]), split(w_a), NT)
+                lba_ref[...] = l_ba
+                l_parts = split(l_ba)
+                s_ref[...] = a_ref[mid:hi, mid:hi] - dot3(l_parts, l_parts, NT)
+
+            @pl.when(index == 2 * j + 1)
+            def _(j=j):
+                finish_pair(j, a_ref, s_ref, w_ref, wa_ref, lba_ref, inv_high_ref, inv_low_ref)
+
+        return carry
+
+    lax.fori_loop(0, B // NB, leaf, 0)
     first_row = B
     first_col = (1 + TR_DEV) * B
 
     def column_strip(i, carry):
-        col_ref[pl.ds(pl.multiple_of(i * STRIP, STRIP), STRIP), :] = panel_strip(first_col + i * STRIP)
+        col_ref[pl.ds(pl.multiple_of(i * STRIP, STRIP), STRIP), :] = panel_strip(left_ref, right_ref, (inv_high_ref, inv_low_ref), first_col + i * STRIP, decay_sq)
         return carry
 
     lax.fori_loop(0, B // STRIP, column_strip, 0)
@@ -273,10 +293,10 @@
             for copy in copies(i - 2):
                 copy.wait()
 
-        panel = panel_strip(first_row + i * STRIP)
+        panel = panel_strip(left_ref, right_ref, (inv_high_ref, inv_low_ref), first_row + i * STRIP, decay_sq)
         panel_buf[slot] = panel
         rows = pl.ds(pl.multiple_of(first_row + i * STRIP, STRIP), STRIP)
-        tile = matern(dot(left_ref[rows, :], right_ref[:, first_col : first_col + B], NN), decay_sq)
+        tile = matern(left_ref, rows, right_ref, slice(first_col, first_col + B), decay_sq)
         row = lax.broadcasted_iota(jnp.int32, (STRIP, B), 0) + i % per_block * STRIP
         col = lax.broadcasted_iota(jnp.int32, (STRIP, B), 1)
         same = blocks_ref[1 + i // per_block] == blocks_ref[1 + TR_DEV]
@@ -308,7 +328,7 @@
     order = jnp.arange(n_blocks, dtype=jnp.int32)
     row_block = (order - 1) * n_prow + me_row + 1
     blocks = jnp.where(order == 0, 0, jnp.where(order <= TR_DEV, row_block, me_col + 1)).astype(jnp.int32)
-    decay_rate = jnp.sqrt(3.0) / length_scale[0]
+    decay_rate = jnp.sqrt(3.0) / length_scale[0] / LN2
     scalars = jnp.stack([decay_rate * decay_rate, noise_var[0]])
     rows = TR_DEV * B
     smem = pl.BlockSpec(memory_space=pltpu.SMEM)
@@ -321,9 +341,7 @@
             pltpu.VMEM((n_blocks * B, 2 * SUB), BF16),
             pltpu.VMEM((2 * SUB, n_blocks * B), BF16),
             pltpu.VMEM((B, B), F32),
-            pltpu.VMEM((NB, NB), F32),
-            pltpu.VMEM((NB, NB), F32),
-            pltpu.VMEM((NB, NB), F32),
+            *[pltpu.VMEM((NB, NB), F32)] * 5,
             pltpu.VMEM((B, B), BF16),
             pltpu.VMEM((B, B), BF16),
             pltpu.VMEM((B, B), BF16),

time: 98.2 us -> 97.9 us (level)
  no operation moved by 1% of the time
where the time goes in v3:
time: 97.9 us; the launch traced here: 97.6 us
  Pallas kernels  80.1 us (82%)
  starting transfers between devices  7.33 us (7%)
  waiting for transfers between devices  5.08 us (5%)
  local copies, waits for them, and re-layouts  2 us (2%)
  between operations  1.98 us (2%)
  other arithmetic  1.16 us (1%)
    pallas_call x1, Pallas kernels, body(): pl.pallas_call(kernel, out_shape=(jax.ShapeDtypeStruct((rows, B), BF16),...  80.1 us
    all_to_all x1, starting transfers between devices, body(): lax.all_to_all(jnp.broadcast_to(mine[None], (devices, width)), ('prow', '...  7.33 us
    all_to_all x1, waiting for transfers between devices, body(): lax.all_to_all(jnp.broadcast_to(mine[None], (devices, width)), ('prow', '...  5.08 us
  transfers between devices with their start and end apart: 1, of which 1 were waited for; matrix products, arithmetic and copies ran while one was open for 1% of the time, Pallas kernels for 0%

profile of v3, /device:TPU:0, one launch (start us, length us, event | category | flops | bytes accessed | tf_op | source)
XLA Modules:
  0.0 97.6 jit_solution(18094961713788108281)
XLA Ops:
  0.6 0.7 pad.4
  1.3 0.7 broadcast_in_dim.13
  2.0 7.3 %all-to-all-start = ((s32[32,1,640]{2,1,0:T(1,128)}), s32[32,1,640]{2,1,0:T(1,128)S(1)}, u32[]{:S(2)}, u32[]{:S(2)}) async-start(s32[32,1,640]{2,1,0:T(1,128)} %broadcast_in_dim.13), calls=%async_computation | async-start | bytes 163840 | tf_op jit(solution)/shard_map/all_to_all | solution.py:323
  10.7 0.7 pad_maximum_fusion.scalars_ref
  11.3 0.5 compare_select_fusion.1.blocks_ref
  11.8 5.1 %all-to-all-done = s32[32,1,640]{2,1,0:T(1,128)S(1)} async-done(((s32[32,1,640]{2,1,0:T(1,128)}), s32[32,1,640]{2,1,0:T(1,128)S(1)}, u32[]{:S(2)}, u32[]{:S(2)}) %all-to-all-start) | async-done | bytes 81952 | tf_op jit(solution)/shard_map/all_to_all | solution.py:323
  16.9 0.6 copy.9
  17.5 80.1 %shard_map.50 = (bf16[4096,1024]{1,0:T(8,128)(2,1)}, bf16[4096,1024]{1,0:T(8,128)(2,1)}) custom-call(s32[6]{0:T(128)} %compare_select_fusion.1.blocks_ref, f32[2]{0:T(128)} %pad_maximum_fusion.scalars_ref, s32[32,640]{1,0:T(8,128)} %bitcast.7), custom_call_target="tpu_custom_call" | custom-call | tf_op jit(solution)/shard_map/pallas_call | solution.py:335
Async XLA Ops:
  2.0 14.9 %all-to-all-start = ((s32[32,1,640]{2,1,0:T(1,128)}), s32[32,1,640]{2,1,0:T(1,128)S(1)}, u32[]{:S(2)}, u32[]{:S(2)}) async-start(s32[32,1,640]{2,1,0:T(1,128)} %broadcast_in_dim.13), calls=%async_computation | async-start | bytes 163840 | tf_op jit(solution)/shard_map/all_to_all | solution.py:323

commit v4 on v3

--- a/solution.py
+++ b/solution.py
@@ -137,42 +137,39 @@
     return z
 
 
+def tree_sum(terms):
+    while len(terms) > 1:
+        terms = [u + v for u, v in zip(terms[::2], terms[1::2])]
+    return terms[0]
+
+
 def factor_block(s_ref, b_ref, w_ref):
     groups = NB // SUB
-    row = lax.broadcasted_iota(jnp.int32, (NB, NB), 0)
-    col = lax.broadcasted_iota(jnp.int32, (NB, NB), 1)
-    b_ref[...] = jnp.where(row == col, 1.0, 0.0)
     lane = lax.broadcasted_iota(jnp.int32, (SUB, LANES), 1)
-    diag = [jnp.where(lax.broadcasted_iota(jnp.int32, (SUB, LANES), 0) == s, 1.0, 0.0) for s in range(SUB)]
+    sub = lax.broadcasted_iota(jnp.int32, (SUB, LANES), 0)
+    diag = [jnp.where(sub == s, 1.0, 0.0) for s in range(SUB)]
     for p in range(groups):
         rows = slice(SUB * p, SUB * (p + 1))
-        s_rows, b_rows = s_ref[rows, :], b_ref[rows, :]
-        e = [lane_of(s_rows, SUB * p + s) for s in range(SUB)]
+        old = s_ref[rows, :]
+        e = [lane_of(old, SUB * p + s) for s in range(SUB)]
         diag = [jnp.where(lane == p, e[s], diag[s]) for s in range(SUB)]
+        block = (lane >= SUB * p) & (lane < SUB * (p + 1))
+        unit = jnp.where(lane == sub + SUB * p, 1.0, 0.0)
+        b_ref[rows, :] = jnp.where(lane < SUB * p, old, unit)
         if p == groups - 1:
             break
-        q_s, q_b = eliminate([s_rows, b_rows], e)
-        q_s = [row_of(q_s, s) for s in range(SUB)]
-        q_b = [row_of(q_b, s) for s in range(SUB)]
+        (q,) = eliminate([jnp.where(block, unit, old)], e)
+        q = [row_of(q, s) for s in range(SUB)]
         for g in range(p + 1, groups):
             other = slice(SUB * g, SUB * (g + 1))
-            s_old, b_old = s_ref[other, :], b_ref[other, :]
-            m = [lane_of(s_old, SUB * p + s) for s in range(SUB)]
-            terms_s = [m[s] * q_s[s] for s in range(SUB)]
-            terms_b = [m[s] * q_b[s] for s in range(SUB)]
-            while len(terms_s) > 1:
-                terms_s = [u + v for u, v in zip(terms_s[::2], terms_s[1::2])]
-                terms_b = [u + v for u, v in zip(terms_b[::2], terms_b[1::2])]
-            s_ref[other, :] = s_old - terms_s[0]
-            b_ref[other, :] = b_old - terms_b[0]
+            old = s_ref[other, :]
+            change = tree_sum([lane_of(old, SUB * p + s) * q[s] for s in range(SUB)])
+            s_ref[other, :] = jnp.where(block, 0.0, old) - change
     factor = small_inverse_factor(diag)
     for p in range(groups):
         rows = slice(SUB * p, SUB * (p + 1))
         b_rows = b_ref[rows, :]
-        terms = [lane_of(factor[s], p) * row_of(b_rows, s) for s in range(SUB)]
-        while len(terms) > 1:
-            terms = [u + v for u, v in zip(terms[::2], terms[1::2])]
-        w_ref[rows, :] = terms[0]
+        w_ref[rows, :] = tree_sum([lane_of(factor[s], p) * row_of(b_rows, s) for s in range(SUB)])
 
 
 def rows_of(parts, start, stop):
@@ -318,10 +315,8 @@
     devices = n_prow * n_pcol
     me_row = lax.axis_index("prow")
     me_col = lax.axis_index("pcol")
-    width = -(-site_code.shape[0] // LANES) * LANES
-    mine = jnp.pad(site_code, (0, width - site_code.shape[0]), constant_values=-1)
     codes = lax.all_to_all(
-        jnp.broadcast_to(mine[None], (devices, width)),
+        jnp.broadcast_to(site_code[None], (devices, site_code.shape[0])),
         ("prow", "pcol"), split_axis=0, concat_axis=0, tiled=True,
     )
     n_blocks = TR_DEV + 1 + SLAB_DEV

time: 97.9 us -> 97.6 us (level)
  no operation moved by 1% of the time
where the time goes in v4:
time: 97.6 us; the launch traced here: 97.3 us
  Pallas kernels  79.8 us (82%)
  starting transfers between devices  7.33 us (8%)
  waiting for transfers between devices  5.08 us (5%)
  local copies, waits for them, and re-layouts  1.99 us (2%)
  between operations  1.98 us (2%)
  other arithmetic  1.16 us (1%)
    pallas_call x1, Pallas kernels, body(): pl.pallas_call(kernel, out_shape=(jax.ShapeDtypeStruct((rows, B), BF16),...  79.8 us
    all_to_all x1, starting transfers between devices, body(): lax.all_to_all(jnp.broadcast_to(site_code[None], (devices, site_code.shap...  7.33 us
    all_to_all x1, waiting for transfers between devices, body(): lax.all_to_all(jnp.broadcast_to(site_code[None], (devices, site_code.shap...  5.08 us
  transfers between devices with their start and end apart: 1, of which 1 were waited for; matrix products, arithmetic and copies ran while one was open for 1% of the time, Pallas kernels for 0%

profile of v4, /device:TPU:0, one launch (start us, length us, event | category | flops | bytes accessed | tf_op | source)
XLA Modules:
  0.0 97.3 jit_solution(16427003413814759293)
XLA Ops:
  0.6 1.4 %broadcast_in_dim.13 = s32[32,1,544]{2,1,0:T(1,128)} broadcast(s32[544]{0:T(1024)} %param.3), dimensions={2} | broadcast | bytes 71808 | tf_op jit(solution)/shard_map/broadcast_in_dim | solution.py:319
  2.0 7.3 %all-to-all-start = ((s32[32,1,544]{2,1,0:T(1,128)}), s32[32,1,544]{2,1,0:T(1,128)S(1)}, u32[]{:S(2)}, u32[]{:S(2)}) async-start(s32[32,1,544]{2,1,0:T(1,128)} %broadcast_in_dim.13), calls=%async_computation | async-start | bytes 163840 | tf_op jit(solution)/shard_map/all_to_all | solution.py:318
  10.7 0.7 pad_maximum_fusion.scalars_ref
  11.3 0.5 compare_select_fusion.1.blocks_ref
  11.8 5.1 %all-to-all-done = s32[32,1,544]{2,1,0:T(1,128)S(1)} async-done(((s32[32,1,544]{2,1,0:T(1,128)}), s32[32,1,544]{2,1,0:T(1,128)S(1)}, u32[]{:S(2)}, u32[]{:S(2)}) %all-to-all-start) | async-done | bytes 69664 | tf_op jit(solution)/shard_map/all_to_all | solution.py:318
  16.9 0.6 copy.9
  17.5 79.8 %shard_map.50 = (bf16[4096,1024]{1,0:T(8,128)(2,1)}, bf16[4096,1024]{1,0:T(8,128)(2,1)}) custom-call(s32[6]{0:T(128)} %compare_select_fusion.1.blocks_ref, f32[2]{0:T(128)} %pad_maximum_fusion.scalars_ref, s32[32,544]{1,0:T(8,128)} %bitcast.7), custom_call_target="tpu_custom_call" | custom-call | tf_op jit(solution)/shard_map/pallas_call | solution.py:330
Async XLA Ops:
  2.0 14.9 %all-to-all-start = ((s32[32,1,544]{2,1,0:T(1,128)}), s32[32,1,544]{2,1,0:T(1,128)S(1)}, u32[]{:S(2)}, u32[]{:S(2)}) async-start(s32[32,1,544]{2,1,0:T(1,128)} %broadcast_in_dim.13), calls=%async_computation | async-start | bytes 163840 | tf_op jit(solution)/shard_map/all_to_all | solution.py:318

commit v5 on v4

--- a/solution.py
+++ b/solution.py
@@ -15,7 +15,7 @@
 SUB = 8
 NB = 128
 PAIR = 2 * NB
-STRIP = 256
+STRIP = 512
 LN2 = 0.6931471805599453
 F32 = jnp.float32
 BF16 = jnp.bfloat16
@@ -231,15 +231,12 @@
     n_blocks = TR_DEV + 1 + SLAB_DEV
     order_sites(codes_ref, blocks_ref, left_ref, right_ref, n_blocks)
 
-    def make_diagonal(i, carry):
-        rows = pl.ds(pl.multiple_of(i * NB, NB), NB)
-        row = lax.broadcasted_iota(jnp.int32, (NB, B), 0) + i * NB
-        col = lax.broadcasted_iota(jnp.int32, (NB, B), 1)
-        tile = matern(left_ref, rows, right_ref, slice(0, B), decay_sq)
-        a_ref[rows, :] = tile + jnp.where(row == col, nugget, 0.0)
-        return carry
-
-    lax.fori_loop(0, B // NB, make_diagonal, 0)
+    for i in range(B // PAIR):
+        lo, hi = i * PAIR, (i + 1) * PAIR
+        row = lax.broadcasted_iota(jnp.int32, (PAIR, hi), 0) + lo
+        col = lax.broadcasted_iota(jnp.int32, (PAIR, hi), 1)
+        tile = matern(left_ref, slice(lo, hi), right_ref, slice(0, hi), decay_sq)
+        a_ref[lo:hi, 0:hi] = tile + jnp.where(row == col, nugget, 0.0)
     s_ref[...] = a_ref[0:NB, 0:NB]
 
     def leaf(index, carry):

time: 97.6 us -> 92.5 us (0.948)
  Pallas kernels: 79.8 us -> 74.6 us
    pallas_call x1, Pallas kernels: 79.8 us -> 74.6 us  [body(): pl.pallas_call(kernel, out_shape=(jax.ShapeDtypeStruct((rows, B), BF16),...]
where the time goes in v5:
time: 92.5 us; the launch traced here: 92.3 us
  Pallas kernels  74.6 us (81%)
  starting transfers between devices  7.33 us (8%)
  waiting for transfers between devices  5.08 us (5%)
  between operations  2.14 us (2%)
  local copies, waits for them, and re-layouts  1.99 us (2%)
  other arithmetic  1.16 us (1%)
    pallas_call x1, Pallas kernels, body(): pl.pallas_call(kernel, out_shape=(jax.ShapeDtypeStruct((rows, B), BF16),...  74.6 us
    all_to_all x1, starting transfers between devices, body(): lax.all_to_all(jnp.broadcast_to(site_code[None], (devices, site_code.shap...  7.33 us
    all_to_all x1, waiting for transfers between devices, body(): lax.all_to_all(jnp.broadcast_to(site_code[None], (devices, site_code.shap...  5.08 us
  transfers between devices with their start and end apart: 1, of which 1 were waited for; matrix products, arithmetic and copies ran while one was open for 1% of the time, Pallas kernels for 0%

profile of v5, /device:TPU:0, one launch (start us, length us, event | category | flops | bytes accessed | tf_op | source)
XLA Modules:
  0.0 92.3 jit_solution(17215605487714600672)
XLA Ops:
  0.6 1.4 %broadcast_in_dim.13 = s32[32,1,544]{2,1,0:T(1,128)} broadcast(s32[544]{0:T(1024)} %param.3), dimensions={2} | broadcast | bytes 71808 | tf_op jit(solution)/shard_map/broadcast_in_dim | solution.py:316
  2.0 7.3 %all-to-all-start = ((s32[32,1,544]{2,1,0:T(1,128)}), s32[32,1,544]{2,1,0:T(1,128)S(1)}, u32[]{:S(2)}, u32[]{:S(2)}) async-start(s32[32,1,544]{2,1,0:T(1,128)} %broadcast_in_dim.13), calls=%async_computation | async-start | bytes 163840 | tf_op jit(solution)/shard_map/all_to_all | solution.py:315
  10.7 0.7 pad_maximum_fusion.scalars_ref
  11.3 0.5 compare_select_fusion.1.blocks_ref
  11.8 5.1 %all-to-all-done = s32[32,1,544]{2,1,0:T(1,128)S(1)} async-done(((s32[32,1,544]{2,1,0:T(1,128)}), s32[32,1,544]{2,1,0:T(1,128)S(1)}, u32[]{:S(2)}, u32[]{:S(2)}) %all-to-all-start) | async-done | bytes 69664 | tf_op jit(solution)/shard_map/all_to_all | solution.py:315
  16.9 0.6 copy.9
  17.5 74.6 %shard_map.50 = (bf16[4096,1024]{1,0:T(8,128)(2,1)}, bf16[4096,1024]{1,0:T(8,128)(2,1)}) custom-call(s32[6]{0:T(128)} %compare_select_fusion.1.blocks_ref, f32[2]{0:T(128)} %pad_maximum_fusion.scalars_ref, s32[32,544]{1,0:T(8,128)} %bitcast.7), custom_call_target="tpu_custom_call" | custom-call | tf_op jit(solution)/shard_map/pallas_call | solution.py:327
Async XLA Ops:
  2.0 14.9 %all-to-all-start = ((s32[32,1,544]{2,1,0:T(1,128)}), s32[32,1,544]{2,1,0:T(1,128)S(1)}, u32[]{:S(2)}, u32[]{:S(2)}) async-start(s32[32,1,544]{2,1,0:T(1,128)} %broadcast_in_dim.13), calls=%async_computation | async-start | bytes 163840 | tf_op jit(solution)/shard_map/all_to_all | solution.py:315

commit v6 on v5

--- a/solution.py
+++ b/solution.py
@@ -15,6 +15,7 @@
 SUB = 8
 NB = 128
 PAIR = 2 * NB
+EARLY = 12
 STRIP = 512
 LN2 = 0.6931471805599453
 F32 = jnp.float32
@@ -165,8 +166,14 @@
             old = s_ref[other, :]
             change = tree_sum([lane_of(old, SUB * p + s) * q[s] for s in range(SUB)])
             s_ref[other, :] = jnp.where(block, 0.0, old) - change
+        if p == EARLY:
+            scale_rows(diag, range(EARLY), b_ref, w_ref)
+    scale_rows(diag, range(EARLY, groups), b_ref, w_ref)
+
+
+def scale_rows(diag, panels, b_ref, w_ref):
     factor = small_inverse_factor(diag)
-    for p in range(groups):
+    for p in panels:
         rows = slice(SUB * p, SUB * (p + 1))
         b_rows = b_ref[rows, :]
         w_ref[rows, :] = tree_sum([lane_of(factor[s], p) * row_of(b_rows, s) for s in range(SUB)])

time: 92.5 us -> 92 us (level)
  no operation moved by 1% of the time
where the time goes in v6:
time: 92 us; the launch traced here: 91.8 us
  Pallas kernels  74.1 us (81%)
  starting transfers between devices  7.33 us (8%)
  waiting for transfers between devices  5.08 us (6%)
  between operations  2.14 us (2%)
  local copies, waits for them, and re-layouts  1.99 us (2%)
  other arithmetic  1.16 us (1%)
    pallas_call x1, Pallas kernels, body(): pl.pallas_call(kernel, out_shape=(jax.ShapeDtypeStruct((rows, B), BF16),...  74.1 us
    all_to_all x1, starting transfers between devices, body(): lax.all_to_all(jnp.broadcast_to(site_code[None], (devices, site_code.shap...  7.33 us
    all_to_all x1, waiting for transfers between devices, body(): lax.all_to_all(jnp.broadcast_to(site_code[None], (devices, site_code.shap...  5.08 us
  transfers between devices with their start and end apart: 1, of which 1 were waited for; matrix products, arithmetic and copies ran while one was open for 1% of the time, Pallas kernels for 0%

profile of v6, /device:TPU:0, one launch (start us, length us, event | category | flops | bytes accessed | tf_op | source)
XLA Modules:
  0.0 91.8 jit_solution(10964900406716971715)
XLA Ops:
  0.6 1.4 %broadcast_in_dim.13 = s32[32,1,544]{2,1,0:T(1,128)} broadcast(s32[544]{0:T(1024)} %param.3), dimensions={2} | broadcast | bytes 71808 | tf_op jit(solution)/shard_map/broadcast_in_dim | solution.py:323
  2.0 7.3 %all-to-all-start = ((s32[32,1,544]{2,1,0:T(1,128)}), s32[32,1,544]{2,1,0:T(1,128)S(1)}, u32[]{:S(2)}, u32[]{:S(2)}) async-start(s32[32,1,544]{2,1,0:T(1,128)} %broadcast_in_dim.13), calls=%async_computation | async-start | bytes 163840 | tf_op jit(solution)/shard_map/all_to_all | solution.py:322
  10.7 0.7 pad_maximum_fusion.scalars_ref
  11.3 0.5 compare_select_fusion.1.blocks_ref
  11.8 5.1 %all-to-all-done = s32[32,1,544]{2,1,0:T(1,128)S(1)} async-done(((s32[32,1,544]{2,1,0:T(1,128)}), s32[32,1,544]{2,1,0:T(1,128)S(1)}, u32[]{:S(2)}, u32[]{:S(2)}) %all-to-all-start) | async-done | bytes 69664 | tf_op jit(solution)/shard_map/all_to_all | solution.py:322
  16.9 0.6 copy.9
  17.5 74.1 %shard_map.50 = (bf16[4096,1024]{1,0:T(8,128)(2,1)}, bf16[4096,1024]{1,0:T(8,128)(2,1)}) custom-call(s32[6]{0:T(128)} %compare_select_fusion.1.blocks_ref, f32[2]{0:T(128)} %pad_maximum_fusion.scalars_ref, s32[32,544]{1,0:T(8,128)} %bitcast.7), custom_call_target="tpu_custom_call" | custom-call | tf_op jit(solution)/shard_map/pallas_call | solution.py:334
Async XLA Ops:
  2.0 14.9 %all-to-all-start = ((s32[32,1,544]{2,1,0:T(1,128)}), s32[32,1,544]{2,1,0:T(1,128)S(1)}, u32[]{:S(2)}, u32[]{:S(2)}) async-start(s32[32,1,544]{2,1,0:T(1,128)} %broadcast_in_dim.13), calls=%async_computation | async-start | bytes 163840 | tf_op jit(solution)/shard_map/all_to_all | solution.py:322
